TPU v7x, 256 devices: a whole 4x4x8 slice. The times are simulated.
256 devices in a mesh: stream: 16 (over y, x), span: 16 (over z, core).
Axes of the slice: x: 4, y: 4, z: 8, core: 2. Of those that a mesh axis runs over, the one named last changes fastest.
Arguments:
- forcing: float32 [5, 512, 512, 128], P(None, 'span', 'stream'), may hold values from -6 to 6
- initial_state: float32 [256, 5, 2, 512, 128], P('span', None, None, 'stream'), may hold values from -4 to 4
- diagonal: float32 [5, 512, 128], replicated, may hold values from 1.5 to 4
- span_speed: float32 [5], replicated, may hold values from 0.3 to 3
- coupling: float32 [4, 5, 5], replicated, may hold values from -1.25 to 1.25
- stiffener_mask: int32 [512, 128], replicated, may hold values 0 or 1
- face_index: int32 [2, 32768], P(None, ('stream', 'span')), may hold values from 0 to 1023
- mode_shapes: float32 [2, 2, 32768], P(None, None, ('stream', 'span')), may hold values from -12 to 12
Outputs:
- flow: float32 [256, 5, 2, 512, 128], P('span', None, None, 'stream')
- forces: float32 [2, 2], replicated
All inputs are finite; a program needn't handle non-finite values.
Results may differ from a plain program's by a relative error of at most 0.00025.
Values sent between devices are 32-bit elements; how exact they have to be, the bound alone decides.
A program may use at most 192 MiB of HBM per device.

v0:
```python
import functools
import math

import jax
import jax.numpy as jnp
import numpy as np
from jax import lax
from jax.experimental import pallas as pl
from jax.experimental.pallas import tpu as pltpu
from jax.sharding import PartitionSpec as P

MESH = pl.DeviceIdType.MESH
S = 16
N = 16
K = 16
C = 5
X = 32
Z = 32
Y = 128
NZ = 512
KR = 2 * K
CHUNKS = X * C // S
f32 = jnp.float32
bf16 = jnp.bfloat16


def table_rows():
    z = np.arange(NZ)
    k = np.arange(NZ // 2)
    phase = (k[:, None] * z[None, :] % NZ) * (2.0 * math.pi / NZ)
    both = np.stack([np.cos(phase), -np.sin(phase)], 0) / math.sqrt(NZ)
    rows = both.reshape(2, S, K, NZ).transpose(1, 0, 2, 3).reshape(NZ, NZ)
    exact = rows.astype(np.float32)
    high = exact.astype(jnp.bfloat16)
    low = (exact - high.astype(np.float32)).astype(jnp.bfloat16)
    return high, low


def split(v):
    high = v.astype(bf16)
    return high, (v - high.astype(f32)).astype(bf16)


def dot3(ah, al, bh, bl):
    d = functools.partial(jnp.dot, preferred_element_type=f32)
    return d(ah, bh) + (d(ah, bl) + d(al, bh))


def cell(order):
    half = lax.div(order, 2)
    return jnp.where(lax.rem(order, 2) == 0, half, X - 1 - half)


def row_of(j, p):
    rho = j * S + p
    return cell(lax.div(rho, C)), lax.rem(rho, C)


def done_after(j):
    return lax.div((j + 1) * S, C)


def loop(lo, hi, body):
    def step(i, carry):
        body(i)
        return carry

    lax.fori_loop(lo, hi, step, 0)


def kernel(
    forcing, init, diag, speed, coup, mask, faces, modes, thigh, tlow,
    flow, forces,
    th, tl, fbuf, sbuf, rhs, q0, q1, q2, near0, alpha, beta, coef, dv, kv, bv,
    fv, mv, wallm, gv, wall, sum1, sum2, fown, mown,
    sem_t, sem_q, sem_d, sem_f, send1, recv1, send2, recv2,
    hs0, hr0, hs1, hr1, fs, fr, ps, pr, osem,
):
    me = lax.axis_index("span")
    st = lax.axis_index("stream")
    first, last = st == 0, st == N - 1
    inner_l, inner_r = st > 0, st < N - 1

    def remote(src, dst, ss, rs, axis, to):
        return pltpu.make_async_remote_copy(
            src_ref=src, dst_ref=dst, send_sem=ss, recv_sem=rs, device_id={axis: to}, device_id_type=MESH
        )

    def arrived(ref, sem):
        pltpu.make_async_copy(ref, ref, sem).wait()

    barrier = pltpu.get_barrier_semaphore()

    def greet(i):
        pl.semaphore_signal(barrier, inc=1, device_id={"span": lax.rem(me + i, S)}, device_id_type=MESH)
        pl.semaphore_signal(barrier, inc=1, device_id={"stream": lax.rem(st + i, N)}, device_id_type=MESH)

    loop(1, S, greet)

    x0 = pl.multiple_of(st * X, X)
    cp_d = pltpu.make_async_copy(diag.at[:, pl.ds(x0, X), :], dv, sem_d.at[0])
    cp_k = pltpu.make_async_copy(mask.at[pl.ds(x0, X), :], kv, sem_d.at[1])
    cp_d.start()
    cp_k.start()
    cp_h = pltpu.make_async_copy(thigh, th, sem_t.at[0])
    cp_l = pltpu.make_async_copy(tlow, tl, sem_t.at[1])
    cp_h.start()
    cp_l.start()
    cp_f = pltpu.make_async_copy(faces, fown, sem_f.at[0])
    cp_m = pltpu.make_async_copy(modes, mown, sem_f.at[1])
    cp_f.start()
    cp_m.start()

    mine = pl.multiple_of(me * Z, Z)

    def own_rows(j):
        x, c = row_of(j, me)
        pltpu.make_async_copy(forcing.at[c, :, x, 0, :], fbuf.at[j, pl.ds(mine, Z), :], recv1.at[j]).start()

    loop(0, CHUNKS, own_rows)

    def load_state(x):
        for c in range(C):
            for r in range(2):
                pltpu.make_async_copy(
                    init.at[:, c, r, x, 0, :], q0.at[x + 1, c, pl.ds(r * K, K), :], sem_q
                ).start()

    loop(0, X, load_state)

    for a in range(4):
        for c in range(C):
            for d in range(C):
                coef[a * 25 + c * 5 + d] = jnp.full((8, Y), coup[a, c, d], f32)
    k_index = (me * K + lax.broadcasted_iota(jnp.int32, (K, Y), 0)).astype(f32)
    for c in range(C):
        bv[c] = k_index * (2.0 * math.pi / NZ) * speed[c]

    @pl.when(first)
    def _():
        q0[0] = jnp.zeros((C, KR, Y), f32)
        q1[0] = jnp.zeros((C, KR, Y), f32)

    @pl.when(last)
    def _():
        q0[X + 1] = jnp.zeros((C, KR, Y), f32)
        q1[X + 1] = jnp.zeros((C, KR, Y), f32)

    cp_f.wait()
    cp_m.wait()
    fv[me] = fown[...]
    mv[me] = mown[...]
    pl.semaphore_wait(barrier, 2 * S - 2)

    def halo0(c):
        for r in range(2):
            rows = pl.ds(r * K, K)

            @pl.when(inner_l)
            def _():
                remote(init.at[:, c, r, 0, 0, :], q0.at[X + 1, c, rows, :], hs0.at[0], hr0.at[1], "stream", st - 1).start()

            @pl.when(inner_r)
            def _():
                remote(init.at[:, c, r, X - 1, 0, :], q0.at[0, c, rows, :], hs0.at[1], hr0.at[0], "stream", st + 1).start()

    loop(0, C, halo0)

    def send_forcing(j):
        def one(i):
            t = lax.rem(me + i, S)
            x, c = row_of(j, t)
            remote(
                forcing.at[c, :, x, 0, :], fbuf.at[j, pl.ds(mine, Z), :], send1, recv1.at[j], "span", t
            ).start()

        loop(1, S, one)

    def send_faces(i):
        t = lax.rem(me + i, S)
        remote(fown, fv.at[me], fs.at[0], fr.at[0], "span", t).start()
        remote(mown, mv.at[me], fs.at[1], fr.at[1], "span", t).start()

    send_forcing(0)
    loop(1, S, send_faces)
    loop(1, CHUNKS, send_forcing)

    cp_d.wait()
    cp_k.wait()

    def factors(x):
        keep = 1.0 - kv[pl.ds(x, 1), :].astype(f32)
        for c in range(C):
            a = jnp.broadcast_to(dv[c, pl.ds(x, 1), :], (K, Y))
            b = bv[c]
            scale = keep / (a * a + b * b)
            alpha[x, c] = a * scale
            beta[x, c] = b * scale

    loop(0, X, factors)

    lane = lax.broadcasted_iota(jnp.int32, (KR, Y), 1)

    def near(q, x):
        acc = [None] * C
        for d in range(C):
            here = q[x + 1, d]
            up = jnp.where(lane < Y - 1, pltpu.roll(here, Y - 1, 1), 0.0)
            down = jnp.where(lane > 0, pltpu.roll(here, 1, 1), 0.0)
            for a, v in enumerate((q[x + 2, d], q[x, d], up, down)):
                v = v.reshape(4, 8, Y)
                for c in range(C):
                    term = coef[a * 25 + c * 5 + d][None] * v
                    acc[c] = term if acc[c] is None else acc[c] + term
        return [v.reshape(KR, Y) for v in acc]

    arrived(q0.at[pl.ds(1, X)], sem_q)

    @pl.when(inner_l)
    def _():
        arrived(q0.at[0], hr0.at[0])

    @pl.when(inner_r)
    def _():
        arrived(q0.at[X + 1], hr0.at[1])

    def first_near(x):
        for c, v in enumerate(near(q0, x)):
            near0[x, c] = v

    loop(0, X, first_near)

    cp_h.wait()
    cp_l.wait()

    def transform(j):
        arrived(fbuf.at[j], recv1.at[j])
        fh, fl = split(fbuf[j])

        def rows(i):
            part = pl.ds(pl.multiple_of(i * 128, 128), 128)
            sbuf[j, part, :] = dot3(th[part, :], tl[part, :], fh, fl)

        for i in range(4):
            rows(i)
        x, c = row_of(j, me)
        rhs[x, c] = sbuf[j, pl.ds(mine, KR), :]

        def one(i):
            t = lax.rem(me + i, S)
            rows_t = pl.ds(pl.multiple_of(t * KR, KR), KR)
            remote(sbuf.at[j, rows_t, :], rhs.at[x, c], send2, recv2.at[j], "span", t).start()

        loop(1, S, one)

    loop(0, CHUNKS, transform)

    arrived(fv.at[pl.ds(0, S - 1)], fr.at[0])
    arrived(mv.at[pl.ds(0, S - 1)], fr.at[1])
    z_row = lax.broadcasted_iota(jnp.int32, (Z, 128), 0)
    x_row = lax.broadcasted_iota(jnp.int32, (128, 128), 0)

    def scatter(s):
        total = jnp.zeros((Z, 128), f32)
        for m in range(2):
            index = fv[s, pl.ds(m, 1), :]
            at_z = z_row == lax.div(index, X)
            for r in range(2):
                placed = (x_row == lax.rem(index, X) + (2 * m + r) * X).astype(f32)
                value = jnp.where(at_z, mv[s, m, pl.ds(r, 1), :], 0.0)
                total = total + lax.dot_general(
                    value, placed, (((1,), (1,)), ((), ())),
                    precision=lax.Precision.HIGHEST, preferred_element_type=f32,
                )
        wallm[pl.ds(pl.multiple_of(s * Z, Z), Z), :] = total

    loop(0, S, scatter)
    wh, wl = split(wallm[...])
    own_k = pl.ds(pl.multiple_of(me * KR, KR), KR)
    row = lax.broadcasted_iota(jnp.int32, (KR, Y), 0)
    zero_k = jnp.logical_and(me == 0, lax.rem(row, K) == 0)
    weight = jnp.where(zero_k, 1.0, 2.0)
    gv[...] = weight * dot3(th[own_k, :], tl[own_k, :], wh, wl)
    wall[...] = jnp.zeros((KR, 128), f32)

    def invert(x, c, d):
        re, im = d[:K], d[K:]
        al, be = alpha[x, c], beta[x, c]
        return al * re + be * im, al * im - be * re

    def sweep1(order):
        x = cell(order)
        for c in range(C):
            re, im = invert(x, c, rhs[x, c] - near0[x, c])
            q1[x + 1, c, 0:K] = re
            q1[x + 1, c, K:KR] = im

    def sweep2(order):
        x = cell(order)
        for c, v in enumerate(near(q1, x)):
            re, im = invert(x, c, rhs[x, c] - v)
            q2[x, c, 0:K] = re
            q2[x, c, K:KR] = im
            if c == C - 1:
                at = jnp.concatenate([re, im], 0)[:, 0:1]
                wall[...] += jnp.where(lax.rem(lane, X) == x, at, 0.0)
        for c in range(C):
            for r in range(2):
                pltpu.make_async_copy(
                    q2.at[x, c, pl.ds(r * K, K), :], flow.at[:, c, r, x, 0, :], osem
                ).start()

    def wait_chunk(j):
        pltpu.make_async_copy(rhs.at[pl.ds(0, 3)], rhs.at[pl.ds(0, 3)], recv2.at[j]).wait()

    wait_chunk(0)
    loop(0, S // C, sweep1)

    @pl.when(inner_l)
    def _():
        remote(q1.at[1], q1.at[X + 1], hs1.at[0], hr1.at[1], "stream", st - 1).start()

    @pl.when(inner_r)
    def _():
        remote(q1.at[X], q1.at[0], hs1.at[1], hr1.at[0], "stream", st + 1).start()

    @pl.when(inner_l)
    def _():
        arrived(q1.at[0], hr1.at[0])

    @pl.when(inner_r)
    def _():
        arrived(q1.at[X + 1], hr1.at[1])

    def chunk(j):
        wait_chunk(j)
        before, now = done_after(j - 1), done_after(j)
        loop(before, now, sweep1)
        loop(jnp.where(j == 1, 0, before - 2), jnp.where(j == CHUNKS - 1, X, now - 2), sweep2)

    loop(1, CHUNKS, chunk)

    part = jnp.sum(wall[...] * gv[...], axis=0, keepdims=True)
    sum1[me] = jnp.broadcast_to(part, (8, 128))
    for phase, (axis, pos, buf) in enumerate((("span", me, sum1), ("stream", st, sum2))):

        def one(i):
            remote(buf.at[pos], buf.at[pos], ps.at[phase], pr.at[phase], axis, lax.rem(pos + i, 16)).start()

        loop(1, 16, one)
        arrived(buf.at[pl.ds(0, 15)], pr.at[phase])
        total = buf[0]
        for i in range(1, 16):
            total = total + buf[i]
        if phase == 0:
            sum2[st] = total
    scale = 1.0 / math.sqrt(256 * 128)
    group = lax.div(lax.broadcasted_iota(jnp.int32, (1, 128), 1), X)
    for m in range(2):
        for r in range(2):
            forces[m, r] = jnp.sum(jnp.where(group == 2 * m + r, total[0:1], 0.0)) * scale

    for phase, buf in enumerate((sum1, sum2)):
        arrived(buf.at[pl.ds(0, 15)], ps.at[phase])
    arrived(fv.at[pl.ds(0, S - 1)], fs.at[0])
    arrived(mv.at[pl.ds(0, S - 1)], fs.at[1])
    arrived(fbuf.at[:, pl.ds(0, NZ - Z), :], send1)
    arrived(sbuf.at[:, pl.ds(0, NZ - Z), :], send2)

    @pl.when(inner_l)
    def _():
        arrived(q0.at[0], hs0.at[0])
        arrived(q1.at[0], hs1.at[0])

    @pl.when(inner_r)
    def _():
        arrived(q0.at[0], hs0.at[1])
        arrived(q1.at[0], hs1.at[1])

    arrived(q2, osem)


def shards(forcing, initial_state, diagonal, span_speed, coupling, stiffener_mask, face_index, mode_shapes):
    high, low = table_rows()
    anyw = pl.BlockSpec(memory_space=pl.ANY)
    smem = pl.BlockSpec(memory_space=pltpu.SMEM)
    vm = pltpu.VMEM
    dma = pltpu.SemaphoreType.DMA
    flow, forces = pl.pallas_call(
        kernel,
        out_shape=(
            jax.ShapeDtypeStruct((K, C, 2, X, 1, Y), f32),
            jax.ShapeDtypeStruct((2, 2), f32),
        ),
        in_specs=[anyw, anyw, anyw, smem, smem, anyw, anyw, anyw, anyw, anyw],
        out_specs=(anyw, smem),
        scratch_shapes=[
            vm((NZ, NZ), bf16), vm((NZ, NZ), bf16),
            vm((CHUNKS, NZ, Y), f32), vm((CHUNKS, NZ, Y), f32),
            vm((X, C, KR, Y), f32),
            vm((X + 2, C, KR, Y), f32), vm((X + 2, C, KR, Y), f32), vm((X, C, KR, Y), f32),
            vm((X, C, KR, Y), f32),
            vm((X, C, K, Y), f32), vm((X, C, K, Y), f32),
            vm((100, 8, Y), f32),
            vm((C, X, Y), f32), vm((X, Y), jnp.int32), vm((C, K, Y), f32),
            vm((S, 2, 128), jnp.int32), vm((S, 2, 2, 128), f32),
            vm((NZ, 128), f32), vm((KR, 128), f32), vm((KR, 128), f32),
            vm((16, 8, 128), f32), vm((16, 8, 128), f32),
            vm((2, 128), jnp.int32), vm((2, 2, 128), f32),
            dma((2,)), dma, dma((2,)), dma((2,)),
            dma, dma((CHUNKS,)), dma, dma((CHUNKS,)),
            dma((2,)), dma((2,)), dma((2,)), dma((2,)),
            dma((2,)), dma((2,)), dma((2,)), dma((2,)), dma,
        ],
        compiler_params=pltpu.CompilerParams(
            collective_id=0, has_side_effects=True, vmem_limit_bytes=64 * 1024 * 1000
        ),
    )(
        forcing.reshape(C, Z, X, 1, Y),
        initial_state.reshape(K, C, 2, X, 1, Y),
        diagonal, span_speed, coupling, stiffener_mask, face_index, mode_shapes,
        jnp.asarray(high), jnp.asarray(low),
    )
    return flow.reshape(K, C, 2, X, Y), forces


def solution(mesh):
    return jax.shard_map(
        shards,
        mesh=mesh,
        in_specs=(
            P(None, "span", "stream", None),
            P("span", None, None, "stream", None),
            P(),
            P(),
            P(),
            P(),
            P(None, ("stream", "span")),
            P(None, None, ("stream", "span")),
        ),
        out_specs=(P("span", None, None, "stream", None), P()),
        check_vma=False,
    )
```

profile of v0, /device:TPU:1, one launch (start us, length us, event | category | flops | bytes accessed | tf_op | source)
XLA Modules:
  0.0 146.9 jit_solution(787648068804698494)
XLA Ops:
  0.6 1.3 copy.12.coup
  1.9 140.7 %shard_map.113 = (f32[16,5,2,32,1,128]{5,4,3,2,1,0:T(1,128)}, f32[2,2]{1,0:T(2,128)}) custom-call(f32[5,32,32,1,128]{4,3,2,1,0:T(1,128)} %bitcast.3, f32[16,5,2,32,1,128]{5,4,3,2,1,0:T(1,128)} %bitcast.4, f32[5,512,128]{2,1,0:T(8,128)} %diag.1, f32[5]{0:T(128)} %speed.1, f32[4,5,5]{2,1,0:T(8,128)} %copy.12.coup, s32[512,128]{1,0:T(8,128)} %mask.1, ...), custom_call_target="tpu_custom_call" | custom-call | tf_op jit(solution)/shard_map/pallas_call | solution.py:389
  142.6 0.0 copy-start
  142.6 3.7 %copy.15 = f32[16,5,2,32,128]{4,3,2,1,0:T(8,128)} copy(f32[16,5,2,32,128]{4,3,2,1,0:T(8,128)} %bitcast.5) | data formatting | bytes 5242880
  146.3 0.0 copy-done
  146.3 0.6 copy.16
Async XLA Ops:
  142.6 3.7 %copy-start = (f32[2,2]{1,0:T(2,128)S(1)}, f32[2,2]{1,0:T(2,128)}, u32[]{:S(2)}) copy-start(f32[2,2]{1,0:T(2,128)} %get-tuple-element.9) | copy-start | bytes 52
where the time goes:
time: 147 us
  Pallas kernels  141 us (96%)
  local copies, waits for them, and re-layouts  5.54 us (4%)
    pallas_call x1, Pallas kernels, shards(): pl.pallas_call(kernel, out_shape=(jax.ShapeDtypeStruct((K, C, 2, X, 1, Y)...  141 us
    unnamed x5, local copies, waits for them, and re-layouts  5.54 us

commit v1 on v0

--- a/solution.py
+++ b/solution.py
@@ -20,6 +20,9 @@
 NZ = 512
 KR = 2 * K
 CHUNKS = X * C // S
+HELD = 7
+EARLY = 2
+MIDDLE = 6
 f32 = jnp.float32
 bf16 = jnp.bfloat16
 
@@ -73,8 +76,9 @@
     flow, forces,
     th, tl, fbuf, sbuf, rhs, q0, q1, q2, near0, alpha, beta, coef, dv, kv, bv,
     fv, mv, wallm, gv, wall, sum1, sum2, fown, mown,
+    wsend, wrecv, rhsw, q1w,
     sem_t, sem_q, sem_d, sem_f, send1, recv1, send2, recv2,
-    hs0, hr0, hs1, hr1, fs, fr, ps, pr, osem,
+    hs0, hr0, hs1, hr1, hs2, hr2, ws, wr, fs, fr, ps, pr, osem,
 ):
     me = lax.axis_index("span")
     st = lax.axis_index("stream")
@@ -131,7 +135,7 @@
     for a in range(4):
         for c in range(C):
             for d in range(C):
-                coef[a * 25 + c * 5 + d] = jnp.full((8, Y), coup[a, c, d], f32)
+                coef[a * 25 + c * 5 + d] = jnp.full((8, Y), coup[c, a, d], f32)
     k_index = (me * K + lax.broadcasted_iota(jnp.int32, (K, Y), 0)).astype(f32)
     for c in range(C):
         bv[c] = k_index * (2.0 * math.pi / NZ) * speed[c]
@@ -140,11 +144,13 @@
     def _():
         q0[0] = jnp.zeros((C, KR, Y), f32)
         q1[0] = jnp.zeros((C, KR, Y), f32)
+        q1w[0] = jnp.zeros((C, KR, Y), f32)
 
     @pl.when(last)
     def _():
         q0[X + 1] = jnp.zeros((C, KR, Y), f32)
         q1[X + 1] = jnp.zeros((C, KR, Y), f32)
+        q1w[X + 1] = jnp.zeros((C, KR, Y), f32)
 
     cp_f.wait()
     cp_m.wait()
@@ -201,17 +207,17 @@
 
     lane = lax.broadcasted_iota(jnp.int32, (KR, Y), 1)
 
-    def near(q, x):
-        acc = [None] * C
+    def near(q, x, outs=tuple(range(C))):
+        acc = [None] * len(outs)
         for d in range(C):
             here = q[x + 1, d]
             up = jnp.where(lane < Y - 1, pltpu.roll(here, Y - 1, 1), 0.0)
             down = jnp.where(lane > 0, pltpu.roll(here, 1, 1), 0.0)
             for a, v in enumerate((q[x + 2, d], q[x, d], up, down)):
                 v = v.reshape(4, 8, Y)
-                for c in range(C):
+                for i, c in enumerate(outs):
                     term = coef[a * 25 + c * 5 + d][None] * v
-                    acc[c] = term if acc[c] is None else acc[c] + term
+                    acc[i] = term if acc[i] is None else acc[i] + term
         return [v.reshape(KR, Y) for v in acc]
 
     arrived(q0.at[pl.ds(1, X)], sem_q)
@@ -236,15 +242,20 @@
     def transform(j):
         arrived(fbuf.at[j], recv1.at[j])
         fh, fl = split(fbuf[j])
-
-        def rows(i):
-            part = pl.ds(pl.multiple_of(i * 128, 128), 128)
-            sbuf[j, part, :] = dot3(th[part, :], tl[part, :], fh, fl)
-
         for i in range(4):
-            rows(i)
+            part = pl.ds(i * 128, 128)
+            value = dot3(th[part, :], tl[part, :], fh, fl)
+            sbuf[j, part, :] = value
+            value = value.reshape(4, 4, 8, Y)
+            for g in range(4):
+                moved = pltpu.roll(value[:, g].reshape(KR, Y), X * g + 2 * j, 1)
+                kept = jnp.where(lax.div(lane, 2) == 16 * g + j, moved, 0.0)
+                wsend[pl.ds(4 * i, 4)] += kept.reshape(4, 8, Y)
         x, c = row_of(j, me)
         rhs[x, c] = sbuf[j, pl.ds(mine, KR), :]
+
+    def send_rows(j):
+        x, c = row_of(j, me)
 
         def one(i):
             t = lax.rem(me + i, S)
@@ -253,7 +264,18 @@
 
         loop(1, S, one)
 
-    loop(0, CHUNKS, transform)
+    wsend[...] = jnp.zeros((S, 8, Y), f32)
+    loop(0, HELD, transform)
+    loop(0, EARLY, send_rows)
+    loop(HELD, CHUNKS, transform)
+    wrecv[me] = wsend[me]
+
+    def send_wall(i):
+        t = lax.rem(me + i, S)
+        remote(wsend.at[t], wrecv.at[me], ws, wr, "span", t).start()
+
+    loop(1, S, send_wall)
+    loop(EARLY, MIDDLE, send_rows)
 
     arrived(fv.at[pl.ds(0, S - 1)], fr.at[0])
     arrived(mv.at[pl.ds(0, S - 1)], fr.at[1])
@@ -301,36 +323,77 @@
             re, im = invert(x, c, rhs[x, c] - v)
             q2[x, c, 0:K] = re
             q2[x, c, K:KR] = im
-            if c == C - 1:
-                at = jnp.concatenate([re, im], 0)[:, 0:1]
-                wall[...] += jnp.where(lax.rem(lane, X) == x, at, 0.0)
         for c in range(C):
             for r in range(2):
                 pltpu.make_async_copy(
                     q2.at[x, c, pl.ds(r * K, K), :], flow.at[:, c, r, x, 0, :], osem
                 ).start()
 
+    def halos(q, hs, hr):
+        @pl.when(inner_l)
+        def _():
+            remote(q.at[1], q.at[X + 1], hs.at[0], hr.at[1], "stream", st - 1).start()
+
+        @pl.when(inner_r)
+        def _():
+            remote(q.at[X], q.at[0], hs.at[1], hr.at[0], "stream", st + 1).start()
+
+        @pl.when(inner_l)
+        def _():
+            arrived(q.at[0], hr.at[0])
+
+        @pl.when(inner_r)
+        def _():
+            arrived(q.at[X + 1], hr.at[1])
+
+    arrived(wrecv.at[pl.ds(0, S - 1)], wr)
+
+    def unpack(p):
+        tile = wrecv[p]
+        for j in range(CHUNKS):
+            x, c = row_of(j, p)
+            for g in range(4):
+                rhsw[x, c, 8 * g : 8 * g + 8] = pltpu.roll(tile, (Y - X * g - 2 * j) % Y, 1)
+            re, im = invert(x, c, rhsw[x, c] - near0[x, c])
+            q1w[x + 1, c, 0:K] = re
+            q1w[x + 1, c, K:KR] = im
+
+    loop(0, S, unpack)
+    halos(q1w, hs2, hr2)
+
+    def wall_values(x):
+        (v,) = near(q1w, x, (C - 1,))
+        re, im = invert(x, C - 1, rhsw[x, C - 1] - v)
+        at = jnp.concatenate([re, im], 0)[:, 0:1]
+        wall[...] += jnp.where(lax.rem(lane, X) == x, at, 0.0)
+
+    loop(0, X, wall_values)
+    part = jnp.sum(wall[...] * gv[...], axis=0, keepdims=True)
+
+    def start_sum(phase, axis, pos, buf):
+        def one(i):
+            remote(buf.at[pos], buf.at[pos], ps.at[phase], pr.at[phase], axis, lax.rem(pos + i, 16)).start()
+
+        loop(1, 16, one)
+
+    def end_sum(phase, buf):
+        arrived(buf.at[pl.ds(0, 15)], pr.at[phase])
+        total = buf[0]
+        for i in range(1, 16):
+            total = total + buf[i]
+        return total
+
+    sum1[me] = jnp.broadcast_to(part, (8, 128))
+    start_sum(0, "span", me, sum1)
+    loop(MIDDLE, CHUNKS, send_rows)
+
     def wait_chunk(j):
         pltpu.make_async_copy(rhs.at[pl.ds(0, 3)], rhs.at[pl.ds(0, 3)], recv2.at[j]).wait()
 
     wait_chunk(0)
     loop(0, S // C, sweep1)
 
-    @pl.when(inner_l)
-    def _():
-        remote(q1.at[1], q1.at[X + 1], hs1.at[0], hr1.at[1], "stream", st - 1).start()
-
-    @pl.when(inner_r)
-    def _():
-        remote(q1.at[X], q1.at[0], hs1.at[1], hr1.at[0], "stream", st + 1).start()
-
-    @pl.when(inner_l)
-    def _():
-        arrived(q1.at[0], hr1.at[0])
-
-    @pl.when(inner_r)
-    def _():
-        arrived(q1.at[X + 1], hr1.at[1])
+    halos(q1, hs1, hr1)
 
     def chunk(j):
         wait_chunk(j)
@@ -338,30 +401,22 @@
         loop(before, now, sweep1)
         loop(jnp.where(j == 1, 0, before - 2), jnp.where(j == CHUNKS - 1, X, now - 2), sweep2)
 
-    loop(1, CHUNKS, chunk)
-
-    part = jnp.sum(wall[...] * gv[...], axis=0, keepdims=True)
-    sum1[me] = jnp.broadcast_to(part, (8, 128))
-    for phase, (axis, pos, buf) in enumerate((("span", me, sum1), ("stream", st, sum2))):
-
-        def one(i):
-            remote(buf.at[pos], buf.at[pos], ps.at[phase], pr.at[phase], axis, lax.rem(pos + i, 16)).start()
-
-        loop(1, 16, one)
-        arrived(buf.at[pl.ds(0, 15)], pr.at[phase])
-        total = buf[0]
-        for i in range(1, 16):
-            total = total + buf[i]
-        if phase == 0:
-            sum2[st] = total
+    loop(1, 6, chunk)
+    sum2[st] = end_sum(0, sum1)
+    start_sum(1, "stream", st, sum2)
+    loop(6, 8, chunk)
+    total = end_sum(1, sum2)
     scale = 1.0 / math.sqrt(256 * 128)
     group = lax.div(lax.broadcasted_iota(jnp.int32, (1, 128), 1), X)
     for m in range(2):
         for r in range(2):
             forces[m, r] = jnp.sum(jnp.where(group == 2 * m + r, total[0:1], 0.0)) * scale
 
+    loop(8, CHUNKS, chunk)
+
     for phase, buf in enumerate((sum1, sum2)):
         arrived(buf.at[pl.ds(0, 15)], ps.at[phase])
+    arrived(wsend.at[pl.ds(0, S - 1)], ws)
     arrived(fv.at[pl.ds(0, S - 1)], fs.at[0])
     arrived(mv.at[pl.ds(0, S - 1)], fs.at[1])
     arrived(fbuf.at[:, pl.ds(0, NZ - Z), :], send1)
@@ -371,11 +426,13 @@
     def _():
         arrived(q0.at[0], hs0.at[0])
         arrived(q1.at[0], hs1.at[0])
+        arrived(q1.at[0], hs2.at[0])
 
     @pl.when(inner_r)
     def _():
         arrived(q0.at[0], hs0.at[1])
         arrived(q1.at[0], hs1.at[1])
+        arrived(q1.at[0], hs2.at[1])
 
     arrived(q2, osem)
 
@@ -389,11 +446,11 @@
     flow, forces = pl.pallas_call(
         kernel,
         out_shape=(
-            jax.ShapeDtypeStruct((K, C, 2, X, 1, Y), f32),
+            pltpu.VMEM((K, C, 2, X, 1, Y), f32),
             jax.ShapeDtypeStruct((2, 2), f32),
         ),
         in_specs=[anyw, anyw, anyw, smem, smem, anyw, anyw, anyw, anyw, anyw],
-        out_specs=(anyw, smem),
+        out_specs=(pl.BlockSpec(memory_space=pltpu.VMEM), smem),
         scratch_shapes=[
             vm((NZ, NZ), bf16), vm((NZ, NZ), bf16),
             vm((CHUNKS, NZ, Y), f32), vm((CHUNKS, NZ, Y), f32),
@@ -407,18 +464,19 @@
             vm((NZ, 128), f32), vm((KR, 128), f32), vm((KR, 128), f32),
             vm((16, 8, 128), f32), vm((16, 8, 128), f32),
             vm((2, 128), jnp.int32), vm((2, 2, 128), f32),
+            vm((S, 8, Y), f32), vm((S, 8, Y), f32), vm((X, C, KR, Y), f32), vm((X + 2, C, KR, Y), f32),
             dma((2,)), dma, dma((2,)), dma((2,)),
             dma, dma((CHUNKS,)), dma, dma((CHUNKS,)),
-            dma((2,)), dma((2,)), dma((2,)), dma((2,)),
+            dma((2,)), dma((2,)), dma((2,)), dma((2,)), dma((2,)), dma((2,)), dma, dma,
             dma((2,)), dma((2,)), dma((2,)), dma((2,)), dma,
         ],
         compiler_params=pltpu.CompilerParams(
-            collective_id=0, has_side_effects=True, vmem_limit_bytes=64 * 1024 * 1000
+            collective_id=0, has_side_effects=True, vmem_limit_bytes=64_350_000
         ),
     )(
         forcing.reshape(C, Z, X, 1, Y),
         initial_state.reshape(K, C, 2, X, 1, Y),
-        diagonal, span_speed, coupling, stiffener_mask, face_index, mode_shapes,
+        diagonal, span_speed, coupling.transpose(1, 0, 2), stiffener_mask, face_index, mode_shapes,
         jnp.asarray(high), jnp.asarray(low),
     )
     return flow.reshape(K, C, 2, X, Y), forces

time: 147 us -> 137 us (0.932)
  Pallas kernels: 141 us -> 134 us
  local copies, waits for them, and re-layouts: 5.54 us -> 2.06 us
    pallas_call x1, Pallas kernels: 141 us -> 134 us  [shards(): pl.pallas_call(kernel, out_shape=(pltpu.VMEM((K, C, 2, X, 1, Y), f32), ja...]
    unnamed x5 -> x4, local copies, waits for them, and re-layouts: 5.54 us -> 2.06 us
where the time goes in v1:
time: 137 us
  Pallas kernels  134 us (98%)
  local copies, waits for them, and re-layouts  2.06 us (2%)
    pallas_call x1, Pallas kernels, shards(): pl.pallas_call(kernel, out_shape=(pltpu.VMEM((K, C, 2, X, 1, Y), f32), ja...  134 us

profile of v1, /device:TPU:1, one launch (start us, length us, event | category | flops | bytes accessed | tf_op | source)
XLA Modules:
  0.0 137.1 jit_solution(18406455421224851236)
XLA Ops:
  0.6 134.4 %shard_map.113 = (f32[16,5,2,32,1,128]{5,4,3,2,1,0:T(1,128)S(1)}, f32[2,2]{1,0:T(2,128)}) custom-call(f32[5,32,32,1,128]{4,3,2,1,0:T(1,128)} %bitcast.5, f32[16,5,2,32,1,128]{5,4,3,2,1,0:T(1,128)} %bitcast.6, f32[5,512,128]{2,1,0:T(8,128)} %diag.1, f32[5]{0:T(128)} %speed.1, f32[5,4,5]{2,1,0:T(4,128)} %bitcast.7, s32[512,128]{1,0:T(8,128)} %mask.1, ...), custom_call_target="tpu_custom_call" | custom-call | tf_op jit(solution)/shard_map/pallas_call | solution.py:446
  135.1 0.0 copy-start
  135.1 1.5 %copy.14 = f32[16,5,2,32,128]{4,3,2,1,0:T(8,128)} copy(f32[16,5,2,32,128]{4,3,2,1,0:T(8,128)S(1)} %bitcast.4) | data formatting | bytes 5242880
  136.6 0.0 copy-done
  136.6 0.6 copy.15
Async XLA Ops:
  135.1 1.5 %copy-start = (f32[2,2]{1,0:T(2,128)S(1)}, f32[2,2]{1,0:T(2,128)}, u32[]{:S(2)}) copy-start(f32[2,2]{1,0:T(2,128)} %get-tuple-element.11) | copy-start | bytes 52

commit v2 on v1

--- a/solution.py
+++ b/solution.py
@@ -63,6 +63,11 @@
     return lax.div((j + 1) * S, C)
 
 
+def far_first(i):
+    half = lax.div(i + 1, 2)
+    return jnp.where(lax.rem(i, 2) == 1, S // 2 - half, S // 2 + half)
+
+
 def loop(lo, hi, body):
     def step(i, carry):
         body(i)
@@ -258,11 +263,11 @@
         x, c = row_of(j, me)
 
         def one(i):
-            t = lax.rem(me + i, S)
+            t = lax.rem(me + far_first(i), S)
             rows_t = pl.ds(pl.multiple_of(t * KR, KR), KR)
             remote(sbuf.at[j, rows_t, :], rhs.at[x, c], send2, recv2.at[j], "span", t).start()
 
-        loop(1, S, one)
+        loop(0, S - 1, one)
 
     wsend[...] = jnp.zeros((S, 8, Y), f32)
     loop(0, HELD, transform)

time: 137 us -> 136 us (level)
    pallas_call x1, Pallas kernels: 134 us -> 133 us  [shards(): pl.pallas_call(kernel, out_shape=(pltpu.VMEM((K, C, 2, X, 1, Y), f32), ja...]
where the time goes in v2:
time: 136 us
  Pallas kernels  133 us (98%)
  local copies, waits for them, and re-layouts  2.06 us (2%)
    pallas_call x1, Pallas kernels, shards(): pl.pallas_call(kernel, out_shape=(pltpu.VMEM((K, C, 2, X, 1, Y), f32), ja...  133 us

profile of v2, /device:TPU:1, one launch (start us, length us, event | category | flops | bytes accessed | tf_op | source)
XLA Modules:
  0.0 135.6 jit_solution(381866676844037250)
XLA Ops:
  0.6 132.9 %shard_map.113 = (f32[16,5,2,32,1,128]{5,4,3,2,1,0:T(1,128)S(1)}, f32[2,2]{1,0:T(2,128)}) custom-call(f32[5,32,32,1,128]{4,3,2,1,0:T(1,128)} %bitcast.5, f32[16,5,2,32,1,128]{5,4,3,2,1,0:T(1,128)} %bitcast.6, f32[5,512,128]{2,1,0:T(8,128)} %diag.1, f32[5]{0:T(128)} %speed.1, f32[5,4,5]{2,1,0:T(4,128)} %bitcast.7, s32[512,128]{1,0:T(8,128)} %mask.1, ...), custom_call_target="tpu_custom_call" | custom-call | tf_op jit(solution)/shard_map/pallas_call | solution.py:451
  133.5 0.0 copy-start
  133.5 1.5 %copy.14 = f32[16,5,2,32,128]{4,3,2,1,0:T(8,128)} copy(f32[16,5,2,32,128]{4,3,2,1,0:T(8,128)S(1)} %bitcast.4) | data formatting | bytes 5242880
  135.0 0.0 copy-done
  135.0 0.6 copy.15
Async XLA Ops:
  133.5 1.5 %copy-start = (f32[2,2]{1,0:T(2,128)S(1)}, f32[2,2]{1,0:T(2,128)}, u32[]{:S(2)}) copy-start(f32[2,2]{1,0:T(2,128)} %get-tuple-element.11) | copy-start | bytes 52

commit v3 on v2

--- a/solution.py
+++ b/solution.py
@@ -20,9 +20,9 @@
 NZ = 512
 KR = 2 * K
 CHUNKS = X * C // S
-HELD = 7
-EARLY = 2
-MIDDLE = 6
+HELD = 8
+EARLY = 1
+MIDDLE = 8
 f32 = jnp.float32
 bf16 = jnp.bfloat16
 
@@ -32,7 +32,7 @@
     k = np.arange(NZ // 2)
     phase = (k[:, None] * z[None, :] % NZ) * (2.0 * math.pi / NZ)
     both = np.stack([np.cos(phase), -np.sin(phase)], 0) / math.sqrt(NZ)
-    rows = both.reshape(2, S, K, NZ).transpose(1, 0, 2, 3).reshape(NZ, NZ)
+    rows = both.reshape(2, S, 2, 8, NZ).transpose(1, 2, 0, 3, 4).reshape(NZ, NZ)
     exact = rows.astype(np.float32)
     high = exact.astype(jnp.bfloat16)
     low = (exact - high.astype(np.float32)).astype(jnp.bfloat16)
@@ -79,11 +79,11 @@
 def kernel(
     forcing, init, diag, speed, coup, mask, faces, modes, thigh, tlow,
     flow, forces,
-    th, tl, fbuf, sbuf, rhs, q0, q1, q2, near0, alpha, beta, coef, dv, kv, bv,
+    th, tl, fbuf, sbuf, rhs, q0, q1, near0, alpha, beta, coef, dv, kv, bv,
     fv, mv, wallm, gv, wall, sum1, sum2, fown, mown,
     wsend, wrecv, rhsw, q1w,
     sem_t, sem_q, sem_d, sem_f, send1, recv1, send2, recv2,
-    hs0, hr0, hs1, hr1, hs2, hr2, ws, wr, fs, fr, ps, pr, osem,
+    hs0, hr0, hs1, hr1, hs2, hr2, ws, wr, fs, fr, ps, pr,
 ):
     me = lax.axis_index("span")
     st = lax.axis_index("stream")
@@ -131,9 +131,10 @@
     def load_state(x):
         for c in range(C):
             for r in range(2):
-                pltpu.make_async_copy(
-                    init.at[:, c, r, x, 0, :], q0.at[x + 1, c, pl.ds(r * K, K), :], sem_q
-                ).start()
+                for h in range(2):
+                    pltpu.make_async_copy(
+                        init.at[pl.ds(8 * h, 8), c, r, x, 0, :], q0.at[x + 1, c, pl.ds(K * h + 8 * r, 8), :], sem_q
+                    ).start()
 
     loop(0, X, load_state)
 
@@ -159,21 +160,25 @@
 
     cp_f.wait()
     cp_m.wait()
-    fv[me] = fown[...]
-    mv[me] = mown[...]
+    core = lax.rem(me, 2)
+    sibling = me + 1 - 2 * core
+    slot = core * (S // 2) + lax.div(me, 2)
+    fv[slot] = fown[...]
+    mv[slot] = mown[...]
     pl.semaphore_wait(barrier, 2 * S - 2)
 
     def halo0(c):
         for r in range(2):
-            rows = pl.ds(r * K, K)
-
-            @pl.when(inner_l)
-            def _():
-                remote(init.at[:, c, r, 0, 0, :], q0.at[X + 1, c, rows, :], hs0.at[0], hr0.at[1], "stream", st - 1).start()
-
-            @pl.when(inner_r)
-            def _():
-                remote(init.at[:, c, r, X - 1, 0, :], q0.at[0, c, rows, :], hs0.at[1], hr0.at[0], "stream", st + 1).start()
+            for h in range(2):
+                rows, ks = pl.ds(K * h + 8 * r, 8), pl.ds(8 * h, 8)
+
+                @pl.when(inner_l)
+                def _():
+                    remote(init.at[ks, c, r, 0, 0, :], q0.at[X + 1, c, rows, :], hs0.at[0], hr0.at[1], "stream", st - 1).start()
+
+                @pl.when(inner_r)
+                def _():
+                    remote(init.at[ks, c, r, X - 1, 0, :], q0.at[0, c, rows, :], hs0.at[1], hr0.at[0], "stream", st + 1).start()
 
     loop(0, C, halo0)
 
@@ -188,12 +193,12 @@
         loop(1, S, one)
 
     def send_faces(i):
-        t = lax.rem(me + i, S)
-        remote(fown, fv.at[me], fs.at[0], fr.at[0], "span", t).start()
-        remote(mown, mv.at[me], fs.at[1], fr.at[1], "span", t).start()
+        t = lax.rem(me + 2 * i, S)
+        remote(fown, fv.at[slot], fs.at[0], fr.at[0], "span", t).start()
+        remote(mown, mv.at[slot], fs.at[1], fr.at[1], "span", t).start()
 
     send_forcing(0)
-    loop(1, S, send_faces)
+    loop(1, S // 2, send_faces)
     loop(1, CHUNKS, send_forcing)
 
     cp_d.wait()
@@ -212,18 +217,18 @@
 
     lane = lax.broadcasted_iota(jnp.int32, (KR, Y), 1)
 
-    def near(q, x, outs=tuple(range(C))):
+    def near(q, x, outs=tuple(range(C)), rows=pl.ds(0, KR)):
         acc = [None] * len(outs)
         for d in range(C):
-            here = q[x + 1, d]
-            up = jnp.where(lane < Y - 1, pltpu.roll(here, Y - 1, 1), 0.0)
-            down = jnp.where(lane > 0, pltpu.roll(here, 1, 1), 0.0)
-            for a, v in enumerate((q[x + 2, d], q[x, d], up, down)):
-                v = v.reshape(4, 8, Y)
+            here = q[x + 1, d, rows]
+            up = jnp.where(lane[: rows.size] < Y - 1, pltpu.roll(here, Y - 1, 1), 0.0)
+            down = jnp.where(lane[: rows.size] > 0, pltpu.roll(here, 1, 1), 0.0)
+            for a, v in enumerate((q[x + 2, d, rows], q[x, d, rows], up, down)):
+                v = v.reshape(rows.size // 8, 8, Y)
                 for i, c in enumerate(outs):
                     term = coef[a * 25 + c * 5 + d][None] * v
                     acc[i] = term if acc[i] is None else acc[i] + term
-        return [v.reshape(KR, Y) for v in acc]
+        return [v.reshape(rows.size, Y) for v in acc]
 
     arrived(q0.at[pl.ds(1, X)], sem_q)
 
@@ -259,6 +264,19 @@
         x, c = row_of(j, me)
         rhs[x, c] = sbuf[j, pl.ds(mine, KR), :]
 
+    def send_half(h):
+        x, c = row_of(CHUNKS - 1, me)
+        rows = pl.ds(K * h, K)
+
+        def one(i):
+            t = lax.rem(me + far_first(i), S)
+            rows_t = pl.ds(pl.multiple_of(t * KR + K * h, K), K)
+            remote(
+                sbuf.at[CHUNKS - 1, rows_t, :], rhs.at[x, c, rows, :], send2, recv2.at[CHUNKS - 1 + h], "span", t
+            ).start()
+
+        loop(0, S - 1, one)
+
     def send_rows(j):
         x, c = row_of(j, me)
 
@@ -272,6 +290,10 @@
     wsend[...] = jnp.zeros((S, 8, Y), f32)
     loop(0, HELD, transform)
     loop(0, EARLY, send_rows)
+    others, same = pl.ds(0, S // 2 - 1), pl.ds(pl.multiple_of(core * (S // 2), S // 2), S // 2)
+    for i, ref in enumerate((fv, mv)):
+        arrived(ref.at[others], fr.at[i])
+        remote(ref.at[same], ref.at[same], fs.at[2 + i], fr.at[2 + i], "span", sibling).start()
     loop(HELD, CHUNKS, transform)
     wrecv[me] = wsend[me]
 
@@ -282,8 +304,8 @@
     loop(1, S, send_wall)
     loop(EARLY, MIDDLE, send_rows)
 
-    arrived(fv.at[pl.ds(0, S - 1)], fr.at[0])
-    arrived(mv.at[pl.ds(0, S - 1)], fr.at[1])
+    arrived(fv.at[same], fr.at[2])
+    arrived(mv.at[same], fr.at[3])
     z_row = lax.broadcasted_iota(jnp.int32, (Z, 128), 0)
     x_row = lax.broadcasted_iota(jnp.int32, (128, 128), 0)
 
@@ -299,40 +321,43 @@
                     value, placed, (((1,), (1,)), ((), ())),
                     precision=lax.Precision.HIGHEST, preferred_element_type=f32,
                 )
-        wallm[pl.ds(pl.multiple_of(s * Z, Z), Z), :] = total
+        place = 2 * lax.rem(s, S // 2) + lax.div(s, S // 2)
+        wallm[pl.ds(pl.multiple_of(place * Z, Z), Z), :] = total
 
     loop(0, S, scatter)
     wh, wl = split(wallm[...])
     own_k = pl.ds(pl.multiple_of(me * KR, KR), KR)
     row = lax.broadcasted_iota(jnp.int32, (KR, Y), 0)
-    zero_k = jnp.logical_and(me == 0, lax.rem(row, K) == 0)
+    zero_k = jnp.logical_and(me == 0, jnp.logical_and(row < K, lax.rem(row, 8) == 0))
     weight = jnp.where(zero_k, 1.0, 2.0)
     gv[...] = weight * dot3(th[own_k, :], tl[own_k, :], wh, wl)
     wall[...] = jnp.zeros((KR, 128), f32)
 
-    def invert(x, c, d):
-        re, im = d[:K], d[K:]
-        al, be = alpha[x, c], beta[x, c]
+    def invert(x, c, d, ks=pl.ds(0, K)):
+        d = d.reshape(ks.size // 8, 2, 8, Y)
+        re, im = d[:, 0], d[:, 1]
+        al = alpha[x, c, ks].reshape(ks.size // 8, 8, Y)
+        be = beta[x, c, ks].reshape(ks.size // 8, 8, Y)
         return al * re + be * im, al * im - be * re
 
-    def sweep1(order):
+    def both(re, im):
+        return jnp.stack([re, im], 1).reshape(-1, Y)
+
+    whole = (pl.ds(0, KR), pl.ds(0, K))
+
+    def sweep1(order, part=whole):
+        rows, ks = part
         x = cell(order)
         for c in range(C):
-            re, im = invert(x, c, rhs[x, c] - near0[x, c])
-            q1[x + 1, c, 0:K] = re
-            q1[x + 1, c, K:KR] = im
-
-    def sweep2(order):
+            q1[x + 1, c, rows] = both(*invert(x, c, rhs[x, c, rows] - near0[x, c, rows], ks))
+
+    def sweep2(order, part=whole):
+        rows, ks = part
         x = cell(order)
-        for c, v in enumerate(near(q1, x)):
-            re, im = invert(x, c, rhs[x, c] - v)
-            q2[x, c, 0:K] = re
-            q2[x, c, K:KR] = im
-        for c in range(C):
-            for r in range(2):
-                pltpu.make_async_copy(
-                    q2.at[x, c, pl.ds(r * K, K), :], flow.at[:, c, r, x, 0, :], osem
-                ).start()
+        for c, v in enumerate(near(q1, x, rows=rows)):
+            for r, u in enumerate(invert(x, c, rhs[x, c, rows] - v, ks)):
+                at = (ks.start * C * 2 + 2 * c + r) * X + x
+                flow[pl.ds(at, ks.size, stride=2 * C * X), :] = u.reshape(ks.size, Y)
 
     def halos(q, hs, hr):
         @pl.when(inner_l)
@@ -359,17 +384,14 @@
             x, c = row_of(j, p)
             for g in range(4):
                 rhsw[x, c, 8 * g : 8 * g + 8] = pltpu.roll(tile, (Y - X * g - 2 * j) % Y, 1)
-            re, im = invert(x, c, rhsw[x, c] - near0[x, c])
-            q1w[x + 1, c, 0:K] = re
-            q1w[x + 1, c, K:KR] = im
+            q1w[x + 1, c] = both(*invert(x, c, rhsw[x, c] - near0[x, c]))
 
     loop(0, S, unpack)
     halos(q1w, hs2, hr2)
 
     def wall_values(x):
         (v,) = near(q1w, x, (C - 1,))
-        re, im = invert(x, C - 1, rhsw[x, C - 1] - v)
-        at = jnp.concatenate([re, im], 0)[:, 0:1]
+        at = both(*invert(x, C - 1, rhsw[x, C - 1] - v))[:, 0:1]
         wall[...] += jnp.where(lax.rem(lane, X) == x, at, 0.0)
 
     loop(0, X, wall_values)
@@ -390,7 +412,9 @@
 
     sum1[me] = jnp.broadcast_to(part, (8, 128))
     start_sum(0, "span", me, sum1)
-    loop(MIDDLE, CHUNKS, send_rows)
+    loop(MIDDLE, CHUNKS - 1, send_rows)
+    send_half(0)
+    send_half(1)
 
     def wait_chunk(j):
         pltpu.make_async_copy(rhs.at[pl.ds(0, 3)], rhs.at[pl.ds(0, 3)], recv2.at[j]).wait()
@@ -404,7 +428,7 @@
         wait_chunk(j)
         before, now = done_after(j - 1), done_after(j)
         loop(before, now, sweep1)
-        loop(jnp.where(j == 1, 0, before - 2), jnp.where(j == CHUNKS - 1, X, now - 2), sweep2)
+        loop(jnp.where(j == 1, 0, before - 2), now - 2, sweep2)
 
     loop(1, 6, chunk)
     sum2[st] = end_sum(0, sum1)
@@ -417,13 +441,23 @@
         for r in range(2):
             forces[m, r] = jnp.sum(jnp.where(group == 2 * m + r, total[0:1], 0.0)) * scale
 
-    loop(8, CHUNKS, chunk)
+    loop(8, CHUNKS - 1, chunk)
+    for h in range(2):
+        part = (pl.ds(K * h, K), pl.ds(8 * h, 8))
+        pltpu.make_async_copy(
+            rhs.at[pl.ds(0, 3), :, pl.ds(0, K), :], rhs.at[pl.ds(0, 3), :, pl.ds(0, K), :], recv2.at[CHUNKS - 1 + h]
+        ).wait()
+        known = (CHUNKS - 1) * S // C
+        loop(known, X, lambda order: sweep1(order, part))
+        loop(known - 2, X, lambda order: sweep2(order, part))
 
     for phase, buf in enumerate((sum1, sum2)):
         arrived(buf.at[pl.ds(0, 15)], ps.at[phase])
     arrived(wsend.at[pl.ds(0, S - 1)], ws)
-    arrived(fv.at[pl.ds(0, S - 1)], fs.at[0])
-    arrived(mv.at[pl.ds(0, S - 1)], fs.at[1])
+    arrived(fv.at[others], fs.at[0])
+    arrived(mv.at[others], fs.at[1])
+    arrived(fv.at[same], fs.at[2])
+    arrived(mv.at[same], fs.at[3])
     arrived(fbuf.at[:, pl.ds(0, NZ - Z), :], send1)
     arrived(sbuf.at[:, pl.ds(0, NZ - Z), :], send2)
 
@@ -438,8 +472,6 @@
         arrived(q0.at[0], hs0.at[1])
         arrived(q1.at[0], hs1.at[1])
         arrived(q1.at[0], hs2.at[1])
-
-    arrived(q2, osem)
 
 
 def shards(forcing, initial_state, diagonal, span_speed, coupling, stiffener_mask, face_index, mode_shapes):
@@ -451,7 +483,7 @@
     flow, forces = pl.pallas_call(
         kernel,
         out_shape=(
-            pltpu.VMEM((K, C, 2, X, 1, Y), f32),
+            pltpu.VMEM((K * C * 2 * X, Y), f32),
             jax.ShapeDtypeStruct((2, 2), f32),
         ),
         in_specs=[anyw, anyw, anyw, smem, smem, anyw, anyw, anyw, anyw, anyw],
@@ -461,7 +493,6 @@
             vm((CHUNKS, NZ, Y), f32), vm((CHUNKS, NZ, Y), f32),
             vm((X, C, KR, Y), f32),
             vm((X + 2, C, KR, Y), f32), vm((X + 2, C, KR, Y), f32), vm((X, C, KR, Y), f32),
-            vm((X, C, KR, Y), f32),
             vm((X, C, K, Y), f32), vm((X, C, K, Y), f32),
             vm((100, 8, Y), f32),
             vm((C, X, Y), f32), vm((X, Y), jnp.int32), vm((C, K, Y), f32),
@@ -471,9 +502,9 @@
             vm((2, 128), jnp.int32), vm((2, 2, 128), f32),
             vm((S, 8, Y), f32), vm((S, 8, Y), f32), vm((X, C, KR, Y), f32), vm((X + 2, C, KR, Y), f32),
             dma((2,)), dma, dma((2,)), dma((2,)),
-            dma, dma((CHUNKS,)), dma, dma((CHUNKS,)),
+            dma, dma((CHUNKS,)), dma, dma((CHUNKS + 1,)),
             dma((2,)), dma((2,)), dma((2,)), dma((2,)), dma((2,)), dma((2,)), dma, dma,
-            dma((2,)), dma((2,)), dma((2,)), dma((2,)), dma,
+            dma((4,)), dma((4,)), dma((2,)), dma((2,)),
         ],
         compiler_params=pltpu.CompilerParams(
             collective_id=0, has_side_effects=True, vmem_limit_bytes=64_350_000

time: 136 us -> 135 us (level)
  no operation moved by 1% of the time
where the time goes in v3:
time: 135 us
  Pallas kernels  132 us (98%)
  local copies, waits for them, and re-layouts  2.06 us (2%)
    pallas_call x1, Pallas kernels, shards(): pl.pallas_call(kernel, out_shape=(pltpu.VMEM((K * C * 2 * X, Y), f32), ja...  132 us

profile of v3, /device:TPU:1, one launch (start us, length us, event | category | flops | bytes accessed | tf_op | source)
XLA Modules:
  0.0 134.8 jit_solution(13119692155473254151)
XLA Ops:
  0.6 132.1 %shard_map.113 = (f32[5120,128]{1,0:T(8,128)S(1)}, f32[2,2]{1,0:T(2,128)}) custom-call(f32[5,32,32,1,128]{4,3,2,1,0:T(1,128)} %bitcast.5, f32[16,5,2,32,1,128]{5,4,3,2,1,0:T(1,128)} %bitcast.6, f32[5,512,128]{2,1,0:T(8,128)} %diag.1, f32[5]{0:T(128)} %speed.1, f32[5,4,5]{2,1,0:T(4,128)} %bitcast.7, s32[512,128]{1,0:T(8,128)} %mask.1, s32[2,128]{1,0:T(2,128)} %faces.1, ...), custom_call_target="tpu_custom_call" | custom-call | tf_op jit(solution)/shard_map/pallas_call | solution.py:483
  132.8 0.0 copy-start
  132.8 1.5 %copy.14 = f32[16,5,2,32,128]{4,3,2,1,0:T(8,128)} copy(f32[16,5,2,32,128]{4,3,2,1,0:T(8,128)S(1)} %bitcast.4) | data formatting | bytes 5242880
  134.3 0.0 copy-done
  134.3 0.6 copy.15
Async XLA Ops:
  132.8 1.5 %copy-start = (f32[2,2]{1,0:T(2,128)S(1)}, f32[2,2]{1,0:T(2,128)}, u32[]{:S(2)}) copy-start(f32[2,2]{1,0:T(2,128)} %get-tuple-element.11) | copy-start | bytes 52

commit v4 on v3

--- a/solution.py
+++ b/solution.py
@@ -22,7 +22,7 @@
 CHUNKS = X * C // S
 HELD = 8
 EARLY = 1
-MIDDLE = 8
+MIDDLE = 7
 f32 = jnp.float32
 bf16 = jnp.bfloat16
 
@@ -184,13 +184,13 @@
 
     def send_forcing(j):
         def one(i):
-            t = lax.rem(me + i, S)
+            t = lax.rem(me + far_first(i), S)
             x, c = row_of(j, t)
             remote(
                 forcing.at[c, :, x, 0, :], fbuf.at[j, pl.ds(mine, Z), :], send1, recv1.at[j], "span", t
             ).start()
 
-        loop(1, S, one)
+        loop(0, S - 1, one)
 
     def send_faces(i):
         t = lax.rem(me + 2 * i, S)

time: 135 us -> 135 us (level)
  no operation moved by 1% of the time
where the time goes in v4:
time: 135 us
  Pallas kernels  132 us (98%)
  local copies, waits for them, and re-layouts  2.06 us (2%)
    pallas_call x1, Pallas kernels, shards(): pl.pallas_call(kernel, out_shape=(pltpu.VMEM((K * C * 2 * X, Y), f32), ja...  132 us

profile of v4, /device:TPU:1, one launch (start us, length us, event | category | flops | bytes accessed | tf_op | source)
XLA Modules:
  0.0 134.8 jit_solution(239654239020113976)
XLA Ops:
  0.6 132.1 %shard_map.113 = (f32[5120,128]{1,0:T(8,128)S(1)}, f32[2,2]{1,0:T(2,128)}) custom-call(f32[5,32,32,1,128]{4,3,2,1,0:T(1,128)} %bitcast.5, f32[16,5,2,32,1,128]{5,4,3,2,1,0:T(1,128)} %bitcast.6, f32[5,512,128]{2,1,0:T(8,128)} %diag.1, f32[5]{0:T(128)} %speed.1, f32[5,4,5]{2,1,0:T(4,128)} %bitcast.7, s32[512,128]{1,0:T(8,128)} %mask.1, s32[2,128]{1,0:T(2,128)} %faces.1, ...), custom_call_target="tpu_custom_call" | custom-call | tf_op jit(solution)/shard_map/pallas_call | solution.py:483
  132.7 0.0 copy-start
  132.7 1.5 %copy.14 = f32[16,5,2,32,128]{4,3,2,1,0:T(8,128)} copy(f32[16,5,2,32,128]{4,3,2,1,0:T(8,128)S(1)} %bitcast.4) | data formatting | bytes 5242880
  134.2 0.0 copy-done
  134.2 0.6 copy.15
Async XLA Ops:
  132.7 1.5 %copy-start = (f32[2,2]{1,0:T(2,128)S(1)}, f32[2,2]{1,0:T(2,128)}, u32[]{:S(2)}) copy-start(f32[2,2]{1,0:T(2,128)} %get-tuple-element.11) | copy-start | bytes 52
